TPU v7x, 32 devices: a whole 2x2x4 slice. The times are simulated.
32 devices in a mesh: groups: 2 (over y), shard: 4 (over z), pair: 4 (over x, core).
Axes of the slice: x: 2, y: 2, z: 4, core: 2. Of those that a mesh axis runs over, the one named last changes fastest.
Arguments:
- gradient: bfloat16 [2, 8, 512, 512], P('groups', None, 'shard'), parts along dimension 0, may hold values from -6.5 to 6.5, as said below
- momentum: bfloat16 [2, 8, 512, 512], P('groups', None, 'shard'), parts along dimension 0, may hold values from -6.5 to 6.5, as said below
Outputs:
- update: bfloat16 [2, 8, 512, 512], P('groups', None, 'shard'), parts along dimension 0
- new_momentum: bfloat16 [2, 8, 512, 512], P('groups', None, 'shard'), parts along dimension 0
There are 2 independent parts, one for each index of `groups`. A program takes and returns all parts, laid end to end along the dimension named above; each array names one. Nothing has to cross between parts.
Inputs may be any that keep to these rules, and one draw needn't show every extreme that they name: `gradient`: entries of order one. `momentum`: entries of order one.
All inputs are finite; a program needn't handle non-finite values.
Results may differ from a plain program's by a relative error of at most 0.0053.
Values may be sent and summed in bfloat16 or wider, within the bound.
A program may use at most 64 MiB of HBM per device.

v0:
```python
import jax
import jax.numpy as jnp
from jax import lax
from jax.sharding import PartitionSpec as P

damping = 0.1
decay_rate = 0.9


def from_partner(value, axis, apart):
    mask = 2**apart
    pairs = [(source, source ^ mask) for source in range(lax.axis_size(axis))]
    return lax.ppermute(value, axis, pairs)


def multiply(left_matrix, right_matrix):
    return jnp.dot(
        left_matrix,
        right_matrix,
        precision=lax.Precision.HIGHEST,
        preferred_element_type=jnp.float32,
    )


def gram_root(gram_matrix):
    block_size = gram_matrix.shape[0]
    identity = jnp.eye(block_size, dtype=jnp.float32)
    scaling = 2.0 * jnp.trace(gram_matrix) / block_size
    root_scale = jnp.sqrt(jnp.sqrt(scaling))
    scaled = gram_matrix / scaling
    leading = (5.0 * identity - scaled) / 4.0
    iterate = leading / root_scale
    squared = multiply(leading, leading)
    fourth = multiply(squared, squared)
    shifted = multiply(fourth, scaled)
    second = (5.0 * identity - shifted) / 4.0
    return multiply(iterate, second)


def local(gradient, momentum):
    new_momentum = (
        decay_rate * momentum.astype(jnp.float32) + gradient.astype(jnp.float32)
    ).astype(jnp.bfloat16)
    block_rows, block_cols, local_rows, block_size = gradient.shape
    half_cols = block_cols // 2
    half_width = block_size // 2
    shards = lax.axis_size("shard")
    position = lax.axis_index("pair")
    column_half = position // 2
    side_index = position % 2
    leading_side = side_index == 0
    grad_half = lax.dynamic_slice_in_dim(gradient, column_half * half_cols, half_cols, 1).reshape(
        shards, local_rows, block_size
    )
    mom_half = lax.dynamic_slice_in_dim(
        new_momentum, column_half * half_cols, half_cols, 1
    ).reshape(shards, local_rows, block_size)
    grad_recv, mom_recv = (
        lax.all_to_all(grad_half, "shard", split_axis=0, concat_axis=1, tiled=True),
        lax.all_to_all(mom_half, "shard", split_axis=0, concat_axis=1, tiled=True),
    )
    grad_block = grad_recv[0]
    mom_block = mom_recv[0]
    identity = jnp.eye(block_size, dtype=jnp.float32)
    oriented = jnp.where(leading_side, grad_block, grad_block.T)
    gram_matrix = (
        jnp.dot(oriented, oriented.T, preferred_element_type=jnp.float32) / block_size
        + damping * identity
    )
    own_root = gram_root(gram_matrix)
    partner = from_partner(own_root, "pair", 0)
    left_root = jnp.where(leading_side, own_root, partner)
    right_root = jnp.where(leading_side, partner, own_root)
    right_part = lax.dynamic_slice_in_dim(right_root, side_index * half_width, half_width, 1)
    partial_prod = multiply(mom_block.astype(jnp.float32), right_part)
    own_piece = multiply(left_root, partial_prod).astype(jnp.bfloat16)
    outgoing = own_piece.reshape(shards, local_rows, half_width)
    returned = lax.all_to_all(outgoing, "shard", split_axis=0, concat_axis=0, tiled=True)
    own_rows = returned.reshape(block_rows, half_cols, local_rows, half_width)
    gathered = lax.all_gather(own_rows[None], "pair", axis=0, tiled=True)
    update = (
        gathered.reshape(2, 2, block_rows, half_cols, local_rows, half_width)
        .transpose(2, 0, 3, 4, 1, 5)
        .reshape(block_rows, block_cols, local_rows, block_size)
    )
    return (update, new_momentum)


def solution(mesh):
    in_specs = (P("groups", None, "shard", None), P("groups", None, "shard", None))
    out_specs = (P("groups", None, "shard", None), P("groups", None, "shard", None))
    return jax.shard_map(local, mesh=mesh, in_specs=in_specs, out_specs=out_specs, check_vma=False)
```

profile of v0, /device:TPU:0, one launch (start us, length us, event | category | flops | bytes accessed | tf_op | source)
XLA Modules:
  0.0 102.2 jit_solution(1875327581618212463)
XLA Ops:
  7.2 1.9 %dynamic-slice_bitcast_fusion.1 = bf16[4,128,512]{2,1,0:T(8,128)(2,1)} fusion(bf16[1,8,128,512]{3,2,1,0:T(8,128)(2,1)} %param.2, s32[]{:T(128)S(6)} %select_n.44), kind=kLoop, calls=%fused_computation.23 | loop fusion | bytes 1048580 | tf_op jit(solution)/shard_map/reshape | solution.py:52
  9.1 6.3 %all-to-all-start = ((bf16[4,128,512]{2,1,0:T(8,128)(2,1)}), bf16[4,128,512]{2,1,0:T(8,128)(2,1)S(1)}, u32[]{:S(2)}, u32[]{:S(2)}) async-start(bf16[4,128,512]{2,1,0:T(8,128)(2,1)} %dynamic-slice_bitcast_fusion.1), calls=%async_computation | async-start | bytes 1048576 | tf_op jit(solution)/shard_map/all_to_all | solution.py:59
  15.4 14.5 %all-to-all-done = bf16[4,128,512]{2,1,0:T(8,128)(2,1)S(1)} async-done(((bf16[4,128,512]{2,1,0:T(8,128)(2,1)}), bf16[4,128,512]{2,1,0:T(8,128)(2,1)S(1)}, u32[]{:S(2)}, u32[]{:S(2)}) %all-to-all-start) | async-done | bytes 524320 | tf_op jit(solution)/shard_map/all_to_all | solution.py:59
  29.9 0.2 copy.12
  30.1 1.1 %select_reduce_fusion = (f32[]{:T(128)}, f32[512,512]{1,0:T(8,128)S(1)}) fusion(bf16[512,512]{1,0:T(8,128)(2,1)S(1)} %bitcast.22, bf16[512,512]{0,1:T(8,128)(2,1)S(1)} %copy.12, pred[]{:T(512)S(6)} %eq.17), kind=kOutput, calls=%fused_computation.11 | convolution fusion | flops 270270464 | bytes 2097157 | tf_op jit(solution)/shard_map/dot_general | solution.py:67
  31.9 2.0 %fusion.6 = f32[512,512]{1,0:T(8,128)S(1)} fusion(f32[512,512]{1,0:T(8,128)S(1)} %get-tuple-element.3, f32[]{:T(128)S(6)} %div.40), kind=kOutput, calls=%fused_computation.13 | convolution fusion | flops 1611923456 | bytes 2097156 | tf_op jit(solution)/shard_map/dot_general | solution.py:17
  33.9 1.8 %fusion.28 = f32[512,512]{1,0:T(8,128)S(1)} fusion(f32[512,512]{1,0:T(8,128)S(1)} %fusion.6), kind=kOutput, calls=%fused_computation.38 | convolution fusion | flops 1610612736 | bytes 2097152 | tf_op jit(solution)/shard_map/dot_general | solution.py:17
  35.7 1.9 %fusion.1 = f32[512,512]{1,0:T(8,128)S(1)} fusion(f32[512,512]{1,0:T(8,128)S(1)} %fusion.28, f32[512,512]{1,0:T(8,128)S(1)} %get-tuple-element.3, f32[]{:T(128)S(6)} %div.40), kind=kOutput, calls=%fused_computation.5 | convolution fusion | flops 1611923456 | bytes 3145732 | tf_op jit(solution)/shard_map/dot_general | solution.py:17
  37.6 0.0 copy-start
  37.7 2.0 %fusion.4 = f32[512,512]{1,0:T(8,128)S(1)} fusion(f32[512,512]{1,0:T(8,128)S(1)} %fusion.1, f32[]{:T(128)S(6)} %sqrt.7, f32[512,512]{1,0:T(8,128)S(1)} %get-tuple-element.3, f32[]{:T(128)S(6)} %div.40), kind=kOutput, calls=%fused_computation.9 | convolution fusion | flops 1612185600 | bytes 3145736 | tf_op jit(solution)/shard_map/dot_general | solution.py:17
  39.7 0.1 collective-permute-start
  39.8 0.4 add_convert_fusion
  40.1 0.9 dynamic-slice_bitcast_fusion
  41.0 0.2 copy-done.1
  41.3 4.1 %all-to-all-start.1 = ((bf16[4,128,512]{2,1,0:T(8,128)(2,1)}), bf16[4,128,512]{2,1,0:T(8,128)(2,1)}, u32[]{:S(2)}, u32[]{:S(2)}) async-start(bf16[4,128,512]{2,1,0:T(8,128)(2,1)} %dynamic-slice_bitcast_fusion), calls=%async_computation.1 | async-start | bytes 1048576 | tf_op jit(solution)/shard_map/all_to_all | solution.py:60
  45.4 0.0 all-gather.3.cloned.1.call-start
  45.5 15.4 %all-to-all-done.1 = bf16[4,128,512]{2,1,0:T(8,128)(2,1)} async-done(((bf16[4,128,512]{2,1,0:T(8,128)(2,1)}), bf16[4,128,512]{2,1,0:T(8,128)(2,1)}, u32[]{:S(2)}, u32[]{:S(2)}) %all-to-all-start.1) | async-done | bytes 524320 | tf_op jit(solution)/shard_map/all_to_all | solution.py:60
  60.9 1.7 %fusion.9 = f32[512,256]{1,0:T(8,128)S(1)} fusion(bf16[512,512]{1,0:T(8,128)(2,1)} %bitcast.4, f32[512,512]{1,0:T(8,128)S(1)} %fusion.4, s32[]{:T(128)S(6)} %select_n.49, f32[512,512]{1,0:T(8,128)S(1)} %collective-permute-done, pred[]{:T(512)S(6)} %eq.17), kind=kOutput, calls=%fused_computation.15 | convolution fusion | flops 805437440 | bytes 2097157 | tf_op jit(solution)/shard_map/dot_general | solution.py:17
  62.6 1.0 convolution_convert_fusion
  63.6 12.0 %all_to_all.23 = bf16[4,128,256]{2,1,0:T(8,128)(2,1)} all-to-all(bf16[4,128,256]{2,1,0:T(8,128)(2,1)S(1)} %bitcast.23), channel_id=1, replica_groups=mesh['groups'=2,'shard'=4,'pair'=4] {'shard'}, dimensions={0} | all-to-all | bytes 524288 | tf_op jit(solution)/shard_map/all_to_all | solution.py:78
  75.6 0.0 all-gather.3.cloned.1.call-update
  75.6 16.0 %all-gather.3.cloned.1.call-done = bf16[16,128,256]{2,1,0:T(8,128)(2,1)} async-done(((bf16[4,128,256]{2,1,0:T(8,128)(2,1)}), bf16[16,128,256]{2,1,0:T(8,128)(2,1)}) %all-gather.3.cloned.1.call-update) | async-done | bytes 1048592 | tf_op jit(solution)/shard_map/all_gather | solution.py:80
  91.6 2.3 %copy.11 = bf16[1,2,4,128,2,256]{5,4,3,2,1,0:T(2,128)(2,1)S(1)} copy(bf16[1,2,4,128,2,256]{5,3,2,4,1,0:T(8,128)(2,1)} %bitcast.24) | data formatting | bytes 2097152 | tf_op jit(solution)/shard_map/transpose | solution.py:83
  93.9 1.5 %reshape.31 = bf16[1,8,128,512]{3,2,1,0:T(8,128)(2,1)} reshape(bf16[1,2,4,128,2,256]{5,4,3,2,1,0:T(2,128)(2,1)S(1)} %copy.11) | data formatting | bytes 2097152 | tf_op jit(solution)/shard_map/reshape | solution.py:84
  (5 shorter events, 0.0 us)
Async XLA Ops:
  9.1 20.8 %all-to-all-start = ((bf16[4,128,512]{2,1,0:T(8,128)(2,1)}), bf16[4,128,512]{2,1,0:T(8,128)(2,1)S(1)}, u32[]{:S(2)}, u32[]{:S(2)}) async-start(bf16[4,128,512]{2,1,0:T(8,128)(2,1)} %dynamic-slice_bitcast_fusion.1), calls=%async_computation | async-start | bytes 1048576 | tf_op jit(solution)/shard_map/all_to_all | solution.py:59
  37.6 2.1 %copy-start = (bf16[1,8,128,512]{3,2,1,0:T(8,128)(2,1)S(1)}, bf16[1,8,128,512]{3,2,1,0:T(8,128)(2,1)}, u32[]{:S(2)}) copy-start(bf16[1,8,128,512]{3,2,1,0:T(8,128)(2,1)} %param.2) | copy-start | bytes 3145732
  37.6 2.1 %copy-start.2 = (bf16[1,8,128,512]{3,2,1,0:T(8,128)(2,1)S(1)}, bf16[1,8,128,512]{3,2,1,0:T(8,128)(2,1)}, u32[]{:S(2)}) copy-start(bf16[1,8,128,512]{3,2,1,0:T(8,128)(2,1)} %param.3) | copy-start | bytes 3145732
  39.7 21.2 %collective-permute-start = (f32[512,512]{1,0:T(8,128)S(1)}, f32[512,512]{1,0:T(8,128)S(1)}, u32[]{:S(2)}, u32[]{:S(2)}) collective-permute-start(f32[512,512]{1,0:T(8,128)S(1)} %fusion.4), channel_id=1, source_target_pairs={{0,1},{1,0},{2,3},{3,2},{4,5},{5,4},{6,7},{7,6},{8,9},{9,8},{10,11... | collective-permute-start | bytes 3145736 | tf_op jit(solution)/shard_map/ppermute | solution.py:13
  40.1 1.1 %copy-start.1 = (bf16[1,8,128,512]{3,2,1,0:T(8,128)(2,1)}, bf16[1,8,128,512]{3,2,1,0:T(8,128)(2,1)S(1)}, u32[]{:S(2)}) copy-start(bf16[1,8,128,512]{3,2,1,0:T(8,128)(2,1)S(1)} %add_convert_fusion) | copy-start | bytes 3145732
  41.3 19.6 %all-to-all-start.1 = ((bf16[4,128,512]{2,1,0:T(8,128)(2,1)}), bf16[4,128,512]{2,1,0:T(8,128)(2,1)}, u32[]{:S(2)}, u32[]{:S(2)}) async-start(bf16[4,128,512]{2,1,0:T(8,128)(2,1)} %dynamic-slice_bitcast_fusion), calls=%async_computation.1 | async-start | bytes 1048576 | tf_op jit(solution)/shard_map/all_to_all | solution.py:60
  45.4 46.2 %all-gather.3.cloned.1.call-start = ((), (), s32[]{:S(2)}) async-start(), calls=%async_computation.3 | async-start | bytes 1310720 | tf_op jit(solution)/shard_map/all_gather | solution.py:80
Sparse Core Ops, SparseCore 0:
  75.7 15.7 all-gather.2
where the time goes:
time: 103 us; the launch traced here: 102 us
  waiting for transfers between devices  45.9 us (45%)
  between operations  14.9 us (14%)
  blocking collectives  12 us (12%)
  matrix products  11.5 us (11%)
  starting transfers between devices  10.6 us (10%)
  local copies, waits for them, and re-layouts  7.03 us (7%)
    all_gather x1, waiting for transfers between devices, local(): gathered = lax.all_gather(own_rows[None], 'pair', axis=0, tiled=True)  16 us
    all_to_all x1, waiting for transfers between devices, local(): lax.all_to_all(mom_half, 'shard', split_axis=0, concat_axis=1, tiled=True)  15.4 us
    all_to_all x1, waiting for transfers between devices, local(): lax.all_to_all(grad_half, 'shard', split_axis=0, concat_axis=1, tiled=True)  14.5 us
    all_to_all x1, blocking collectives, local(): lax.all_to_all(outgoing, 'shard', split_axis=0, concat_axis=0, tiled=True)  12 us
    dot_general x6, matrix products, multiply(): jnp.dot(left_matrix, right_matrix, precision=lax.Precision.HIGHEST, prefe...  10.4 us
    all_to_all x1, starting transfers between devices, local(): lax.all_to_all(grad_half, 'shard', split_axis=0, concat_axis=1, tiled=True)  6.35 us
    all_to_all x1, starting transfers between devices, local(): lax.all_to_all(mom_half, 'shard', split_axis=0, concat_axis=1, tiled=True)  4.14 us
    transpose x1, local copies, waits for them, and re-layouts, local(): update = gathered.reshape(2, 2, block_rows, half_cols, local_rows, half_w...  2.3 us
  transfers between devices with their start and end apart: 4, of which 3 were waited for; matrix products, arithmetic and copies ran while one was open for 1% of the time, Pallas kernels for 0%

commit v1 on v0

--- a/solution.py
+++ b/solution.py
@@ -77,7 +77,15 @@
     outgoing = own_piece.reshape(shards, local_rows, half_width)
     returned = lax.all_to_all(outgoing, "shard", split_axis=0, concat_axis=0, tiled=True)
     own_rows = returned.reshape(block_rows, half_cols, local_rows, half_width)
-    gathered = lax.all_gather(own_rows[None], "pair", axis=0, tiled=True)
+    part = own_rows[None]
+    count = lax.axis_size("pair")
+    right = [(i, (i + 1) % count) for i in range(count)]
+    parts = [part]
+    for far in range(1, count):
+        parts = [lax.ppermute(parts[0], "pair", right), *parts]
+    full = jnp.concatenate(parts, axis=0)
+    shift = (lax.axis_index("pair") + 1) * parts[-1].shape[0]
+    gathered = jnp.roll(full, shift, axis=0)
     update = (
         gathered.reshape(2, 2, block_rows, half_cols, local_rows, half_width)
         .transpose(2, 0, 3, 4, 1, 5)

time: 103 us -> 88.3 us (0.86)
  between operations: 14.9 us -> 1.59 us
  local copies, waits for them, and re-layouts: 7.03 us -> 5.24 us
  waiting for transfers between devices: 45.9 us -> 47.3 us
    ppermute x0 -> x3, waiting for transfers between devices: none -> 17.4 us  [local(): parts = [lax.ppermute(parts[0], 'pair', right), *parts]]
    all_gather x1 -> x0, waiting for transfers between devices: 16 us -> none  [local(): gathered = lax.all_gather(own_rows[None], 'pair', axis=0, tiled=True)]
    transpose x1, local copies, waits for them, and re-layouts: 2.3 us -> 0.66 us  [local(): update = gathered.reshape(2, 2, block_rows, half_cols, local_rows, half_w...]
    reshape x1 -> x0, local copies, waits for them, and re-layouts: 1.49 us -> none  [local(): update = gathered.reshape(2, 2, block_rows, half_cols, local_rows, half_w...]
    unnamed x6 -> x14, local copies, waits for them, and re-layouts: 0.26 us -> 1.47 us
  transfers between devices with their start and end apart: 4 -> 6, of which waited for: 3 -> 5; matrix products, arithmetic and copies ran while one was open for 1% -> 1% of each run, Pallas kernels for 0% -> 0%
where the time goes in v1:
time: 88.3 us; the launch traced here: 87.9 us
  waiting for transfers between devices  47.3 us (54%)
  matrix products  11.5 us (13%)
  blocking collectives  11.3 us (13%)
  starting transfers between devices  10.6 us (12%)
  local copies, waits for them, and re-layouts  5.24 us (6%)
  between operations  1.59 us (2%)
    ppermute x3, waiting for transfers between devices, local(): parts = [lax.ppermute(parts[0], 'pair', right), *parts]  17.4 us
    all_to_all x1, waiting for transfers between devices, local(): lax.all_to_all(mom_half, 'shard', split_axis=0, concat_axis=1, tiled=True)  15.5 us
    all_to_all x1, waiting for transfers between devices, local(): lax.all_to_all(grad_half, 'shard', split_axis=0, concat_axis=1, tiled=True)  14.5 us
    all_to_all x1, blocking collectives, local(): lax.all_to_all(outgoing, 'shard', split_axis=0, concat_axis=0, tiled=True)  11.3 us
    dot_general x6, matrix products, multiply(): jnp.dot(left_matrix, right_matrix, precision=lax.Precision.HIGHEST, prefe...  10.4 us
    all_to_all x1, starting transfers between devices, local(): lax.all_to_all(grad_half, 'shard', split_axis=0, concat_axis=1, tiled=True)  6.35 us
    all_to_all x1, starting transfers between devices, local(): lax.all_to_all(mom_half, 'shard', split_axis=0, concat_axis=1, tiled=True)  4.14 us
    reshape x1, local copies, waits for them, and re-layouts, local(): lax.dynamic_slice_in_dim(gradient, column_half * half_cols, half_cols, 1)  1.87 us
  transfers between devices with their start and end apart: 6, of which 5 were waited for; matrix products, arithmetic and copies ran while one was open for 1% of the time, Pallas kernels for 0%

profile of v1, /device:TPU:0, one launch (start us, length us, event | category | flops | bytes accessed | tf_op | source)
XLA Modules:
  0.0 87.9 jit_solution(2651183138997968309)
XLA Ops:
  0.6 1.9 %dynamic-slice_bitcast_fusion.1 = bf16[4,128,512]{2,1,0:T(8,128)(2,1)} fusion(bf16[1,8,128,512]{3,2,1,0:T(8,128)(2,1)} %param.2, s32[]{:T(128)S(6)} %select_n.56), kind=kLoop, calls=%fused_computation.23 | loop fusion | bytes 1048580 | tf_op jit(solution)/shard_map/reshape | solution.py:52
  2.5 6.3 %all-to-all-start = ((bf16[4,128,512]{2,1,0:T(8,128)(2,1)}), bf16[4,128,512]{2,1,0:T(8,128)(2,1)S(1)}, u32[]{:S(2)}, u32[]{:S(2)}) async-start(bf16[4,128,512]{2,1,0:T(8,128)(2,1)} %dynamic-slice_bitcast_fusion.1), calls=%async_computation | async-start | bytes 1048576 | tf_op jit(solution)/shard_map/all_to_all | solution.py:59
  8.9 14.5 %all-to-all-done = bf16[4,128,512]{2,1,0:T(8,128)(2,1)S(1)} async-done(((bf16[4,128,512]{2,1,0:T(8,128)(2,1)}), bf16[4,128,512]{2,1,0:T(8,128)(2,1)S(1)}, u32[]{:S(2)}, u32[]{:S(2)}) %all-to-all-start) | async-done | bytes 524320 | tf_op jit(solution)/shard_map/all_to_all | solution.py:59
  23.4 0.2 copy.11
  23.6 1.1 %select_reduce_fusion = (f32[]{:T(128)}, f32[512,512]{1,0:T(8,128)S(1)}) fusion(bf16[512,512]{1,0:T(8,128)(2,1)S(1)} %bitcast.29, bf16[512,512]{0,1:T(8,128)(2,1)S(1)} %copy.11, pred[]{:T(512)S(6)} %eq.20), kind=kOutput, calls=%fused_computation.11 | convolution fusion | flops 270270464 | bytes 2097157 | tf_op jit(solution)/shard_map/dot_general | solution.py:67
  25.4 2.0 %fusion.6 = f32[512,512]{1,0:T(8,128)S(1)} fusion(f32[512,512]{1,0:T(8,128)S(1)} %get-tuple-element.5, f32[]{:T(128)S(6)} %div.40), kind=kOutput, calls=%fused_computation.13 | convolution fusion | flops 1611923456 | bytes 2097156 | tf_op jit(solution)/shard_map/dot_general | solution.py:17
  27.4 1.8 %fusion.28 = f32[512,512]{1,0:T(8,128)S(1)} fusion(f32[512,512]{1,0:T(8,128)S(1)} %fusion.6), kind=kOutput, calls=%fused_computation.47 | convolution fusion | flops 1610612736 | bytes 2097152 | tf_op jit(solution)/shard_map/dot_general | solution.py:17
  29.2 1.9 %fusion.1 = f32[512,512]{1,0:T(8,128)S(1)} fusion(f32[512,512]{1,0:T(8,128)S(1)} %fusion.28, f32[512,512]{1,0:T(8,128)S(1)} %get-tuple-element.5, f32[]{:T(128)S(6)} %div.40), kind=kOutput, calls=%fused_computation.5 | convolution fusion | flops 1611923456 | bytes 3145732 | tf_op jit(solution)/shard_map/dot_general | solution.py:17
  31.1 0.0 copy-start
  31.1 2.0 %fusion.4 = f32[512,512]{1,0:T(8,128)S(1)} fusion(f32[512,512]{1,0:T(8,128)S(1)} %fusion.1, f32[]{:T(128)S(6)} %sqrt.7, f32[512,512]{1,0:T(8,128)S(1)} %get-tuple-element.5, f32[]{:T(128)S(6)} %div.40), kind=kOutput, calls=%fused_computation.9 | convolution fusion | flops 1612185600 | bytes 3145736 | tf_op jit(solution)/shard_map/dot_general | solution.py:17
  33.1 0.1 collective-permute-start
  33.2 0.4 add_convert_fusion
  33.6 0.9 %dynamic-slice_bitcast_fusion = bf16[4,128,512]{2,1,0:T(8,128)(2,1)} fusion(bf16[1,8,128,512]{3,2,1,0:T(8,128)(2,1)S(1)} %add_convert_fusion, s32[]{:T(128)S(6)} %select_n.56), kind=kLoop, calls=%fused_computation.18 | loop fusion | bytes 1048580 | tf_op jit(solution)/shard_map/reshape | solution.py:57
  34.5 4.1 %all-to-all-start.1 = ((bf16[4,128,512]{2,1,0:T(8,128)(2,1)}), bf16[4,128,512]{2,1,0:T(8,128)(2,1)}, u32[]{:S(2)}, u32[]{:S(2)}) async-start(bf16[4,128,512]{2,1,0:T(8,128)(2,1)} %dynamic-slice_bitcast_fusion), calls=%async_computation.1 | async-start | bytes 1048576 | tf_op jit(solution)/shard_map/all_to_all | solution.py:60
  38.7 15.5 %all-to-all-done.1 = bf16[4,128,512]{2,1,0:T(8,128)(2,1)} async-done(((bf16[4,128,512]{2,1,0:T(8,128)(2,1)}), bf16[4,128,512]{2,1,0:T(8,128)(2,1)}, u32[]{:S(2)}, u32[]{:S(2)}) %all-to-all-start.1) | async-done | bytes 524320 | tf_op jit(solution)/shard_map/all_to_all | solution.py:60
  54.1 1.7 %fusion.9 = f32[512,256]{1,0:T(8,128)S(1)} fusion(bf16[512,512]{1,0:T(8,128)(2,1)} %bitcast.4, f32[512,512]{1,0:T(8,128)S(1)} %fusion.4, s32[]{:T(128)S(6)} %select_n.61, f32[512,512]{1,0:T(8,128)S(1)} %collective-permute-done, pred[]{:T(512)S(6)} %eq.20), kind=kOutput, calls=%fused_computation.15 | convolution fusion | flops 805437440 | bytes 2097157 | tf_op jit(solution)/shard_map/dot_general | solution.py:17
  55.9 1.0 %convolution_convert_fusion = bf16[512,256]{1,0:T(8,128)(2,1)S(1)} fusion(f32[512,256]{1,0:T(8,128)S(1)} %fusion.9, f32[512,512]{1,0:T(8,128)S(1)} %fusion.4, f32[512,512]{1,0:T(8,128)S(1)} %collective-permute-done, pred[]{:T(512)S(6)} %eq.20), kind=kOutput, calls=%fused_computation.6 | convolution fusion | flops 805699584 | bytes 2883585 | tf_op jit(solution)/shard_map/dot_general | solution.py:17
  56.9 11.3 %all_to_all.23 = bf16[4,128,256]{2,1,0:T(8,128)(2,1)S(1)} all-to-all(bf16[4,128,256]{2,1,0:T(8,128)(2,1)S(1)} %bitcast.30), channel_id=1, replica_groups=mesh['groups'=2,'shard'=4,'pair'=4] {'shard'}, dimensions={0} | all-to-all | bytes 524288 | tf_op jit(solution)/shard_map/all_to_all | solution.py:78
  68.2 5.8 %collective-permute-done.1 = bf16[1,1,4,128,256]{4,3,2,0,1:T(8,128)(2,1)S(1)} collective-permute-done((bf16[1,1,4,128,256]{4,3,2,0,1:T(8,128)(2,1)S(1)}, bf16[1,1,4,128,256]{4,3,2,0,1:T(8,128)(2,1)S(1)}, u32[]{:S(2)}, u32[]{:S(2)}) %collective-permute-start.1) | collective-permute-done | bytes 262176 | tf_op jit(solution)/shard_map/ppermute | solution.py:85
  74.0 5.8 %collective-permute-done.2 = bf16[1,1,4,128,256]{4,3,2,0,1:T(8,128)(2,1)S(1)} collective-permute-done((bf16[1,1,4,128,256]{4,3,2,0,1:T(8,128)(2,1)S(1)}, bf16[1,1,4,128,256]{4,3,2,0,1:T(8,128)(2,1)S(1)}, u32[]{:S(2)}, u32[]{:S(2)}) %collective-permute-start.2) | collective-permute-done | bytes 262176 | tf_op jit(solution)/shard_map/ppermute | solution.py:85
  79.8 5.8 %collective-permute-done.3 = bf16[1,1,4,128,256]{4,3,2,0,1:T(8,128)(2,1)S(1)} collective-permute-done((bf16[1,1,4,128,256]{4,3,2,0,1:T(8,128)(2,1)S(1)}, bf16[1,1,4,128,256]{4,3,2,0,1:T(8,128)(2,1)S(1)}, u32[]{:S(2)}, u32[]{:S(2)}) %collective-permute-start.3) | collective-permute-done | bytes 262176 | tf_op jit(solution)/shard_map/ppermute | solution.py:85
  85.8 0.1 constant_dynamic-slice_fusion
  85.9 0.7 copy.9
  86.6 1.3 %copy.10 = bf16[1,8,128,512]{3,2,1,0:T(8,128)(2,1)} copy(bf16[1,8,128,512]{2,3,1,0:T(8,128)(2,1)S(1)} %bitcast.26) | data formatting | bytes 2097152
  (17 shorter events, 0.2 us)
Async XLA Ops:
  2.5 20.8 %all-to-all-start = ((bf16[4,128,512]{2,1,0:T(8,128)(2,1)}), bf16[4,128,512]{2,1,0:T(8,128)(2,1)S(1)}, u32[]{:S(2)}, u32[]{:S(2)}) async-start(bf16[4,128,512]{2,1,0:T(8,128)(2,1)} %dynamic-slice_bitcast_fusion.1), calls=%async_computation | async-start | bytes 1048576 | tf_op jit(solution)/shard_map/all_to_all | solution.py:59
  31.1 2.1 %copy-start = (bf16[1,8,128,512]{3,2,1,0:T(8,128)(2,1)S(1)}, bf16[1,8,128,512]{3,2,1,0:T(8,128)(2,1)}, u32[]{:S(2)}) copy-start(bf16[1,8,128,512]{3,2,1,0:T(8,128)(2,1)} %param.2) | copy-start | bytes 3145732
  31.1 2.1 %copy-start.2 = (bf16[1,8,128,512]{3,2,1,0:T(8,128)(2,1)S(1)}, bf16[1,8,128,512]{3,2,1,0:T(8,128)(2,1)}, u32[]{:S(2)}) copy-start(bf16[1,8,128,512]{3,2,1,0:T(8,128)(2,1)} %param.3) | copy-start | bytes 3145732
  33.1 21.0 %collective-permute-start = (f32[512,512]{1,0:T(8,128)S(1)}, f32[512,512]{1,0:T(8,128)S(1)}, u32[]{:S(2)}, u32[]{:S(2)}) collective-permute-start(f32[512,512]{1,0:T(8,128)S(1)} %fusion.4), channel_id=1, source_target_pairs={{0,1},{1,0},{2,3},{3,2},{4,5},{5,4},{6,7},{7,6},{8,9},{9,8},{10,11... | collective-permute-start | bytes 3145736 | tf_op jit(solution)/shard_map/ppermute | solution.py:13
  33.6 22.3 %copy-start.1 = (bf16[1,8,128,512]{3,2,1,0:T(8,128)(2,1)}, bf16[1,8,128,512]{3,2,1,0:T(8,128)(2,1)S(1)}, u32[]{:S(2)}) copy-start(bf16[1,8,128,512]{3,2,1,0:T(8,128)(2,1)S(1)} %add_convert_fusion) | copy-start | bytes 3145732
  34.5 19.6 %all-to-all-start.1 = ((bf16[4,128,512]{2,1,0:T(8,128)(2,1)}), bf16[4,128,512]{2,1,0:T(8,128)(2,1)}, u32[]{:S(2)}, u32[]{:S(2)}) async-start(bf16[4,128,512]{2,1,0:T(8,128)(2,1)} %dynamic-slice_bitcast_fusion), calls=%async_computation.1 | async-start | bytes 1048576 | tf_op jit(solution)/shard_map/all_to_all | solution.py:60
  68.2 5.8 %collective-permute-start.1 = (bf16[1,1,4,128,256]{4,3,2,0,1:T(8,128)(2,1)S(1)}, bf16[1,1,4,128,256]{4,3,2,0,1:T(8,128)(2,1)S(1)}, u32[]{:S(2)}, u32[]{:S(2)}) collective-permute-start(bf16[1,1,4,128,256]{4,3,2,0,1:T(8,128)(2,1)S(1)} %bitcast.27), channel_id=1, source_target_pairs={{0,1},{1,2},{2,3},{3,0},{4,5},{5,6},{6,7},{7,4},{8,9},{9,10},{10,1... | collective-permute-start | bytes 786440 | tf_op jit(solution)/shard_map/ppermute | solution.py:85
  74.0 5.8 %collective-permute-start.2 = (bf16[1,1,4,128,256]{4,3,2,0,1:T(8,128)(2,1)S(1)}, bf16[1,1,4,128,256]{4,3,2,0,1:T(8,128)(2,1)S(1)}, u32[]{:S(2)}, u32[]{:S(2)}) collective-permute-start(bf16[1,1,4,128,256]{4,3,2,0,1:T(8,128)(2,1)S(1)} %collective-permute-done.1), channel_id=1, source_target_pairs={{0,1},{1,2},{2,3},{3,0},{4,5},{5,6},{6,7},{7,4},{8,9},{9,10},{10,1... | collective-permute-start | bytes 786440 | tf_op jit(solution)/shard_map/ppermute | solution.py:85
  79.8 5.8 %collective-permute-start.3 = (bf16[1,1,4,128,256]{4,3,2,0,1:T(8,128)(2,1)S(1)}, bf16[1,1,4,128,256]{4,3,2,0,1:T(8,128)(2,1)S(1)}, u32[]{:S(2)}, u32[]{:S(2)}) collective-permute-start(bf16[1,1,4,128,256]{4,3,2,0,1:T(8,128)(2,1)S(1)} %collective-permute-done.2), channel_id=1, source_target_pairs={{0,1},{1,2},{2,3},{3,0},{4,5},{5,6},{6,7},{7,4},{8,9},{9,10},{10,1... | collective-permute-start | bytes 786440 | tf_op jit(solution)/shard_map/ppermute | solution.py:85
